TPU v7x, 128 devices: a whole 4x4x4 slice. The times are simulated.
128 devices in a mesh: bin: 4 (over y), grp: 32 (over x, z, core).
Axes of the slice: x: 4, y: 4, z: 4, core: 2. Of those that a mesh axis runs over, the one named last changes fastest.
Arguments:
- templates: bfloat16 [131072, 512], P(('bin', 'grp')), may hold values from -6 to 6
- owner_device: int32 [131072, 1], P(('bin', 'grp')), may hold values from 0 to 127; in each aligned block of 1024 rows (0 to 1023, 1024 to 2047, ...) at most 16 rows name the same one
- rate_code: int32 [131072], P(('bin', 'grp')), may hold values from 0 to 4
- rate_gains: float32 [5, 512], replicated, may hold values from 0.5 to 2
- sketch: float32 [512, 256], replicated, may hold values from -6 to 6
- strain: float32 [2, 262144], P(None, 'grp'), may hold values from -6 to 6
Outputs:
- mixing: bfloat16 [131072, 256], P(('bin', 'grp'))
- spectrum: float32 [4, 256], P('bin')
- filtered_0: bfloat16 [4, 2, 262144, 256], P('bin', None, 'grp')
- filtered_1: bfloat16 [4, 2, 131072, 256], P('bin', None, 'grp')
- filtered_2: bfloat16 [4, 2, 65536, 256], P('bin', None, 'grp')
- filtered_3: bfloat16 [4, 2, 32768, 256], P('bin', None, 'grp')
- filtered_4: bfloat16 [4, 2, 16384, 256], P('bin', None, 'grp')
Inputs may be any that keep to these rules, and one draw needn't show every extreme that they name: `owner_device`: among the rows of one device, no device is named by more than 16 rows, and some device is named by exactly 16 rows.
All inputs are finite; a program needn't handle non-finite values.
Results may differ from a plain program's by a relative error of at most 0.0059.
Values may be sent and summed in bfloat16 or wider, within the bound.
A program may use at most 128 MiB of HBM per device.

v0:
```python
import math
import jax
import jax.numpy as jnp
from jax import lax
from jax.sharding import PartitionSpec as P

highest = lax.Precision.HIGHEST
inv_root_two = 0.7071067811865476


def shifted(x, axis, by):
    length = lax.axis_size(axis)
    pairs = [(i, i + by) for i in range(length) if 0 <= i + by < length]
    return lax.ppermute(x, axis, pairs)


def whiten_rows(templates, rate_code, rate_gains):
    factor = jnp.zeros(templates.shape, jnp.float32)
    for rate_level in range(rate_gains.shape[0]):
        factor = factor + jnp.where(
            (rate_code == rate_level)[:, None], rate_gains[rate_level][None, :], jnp.float32(0.0)
        )
    return (templates.astype(jnp.float32) * factor).astype(jnp.bfloat16)


def strain_levels(strain, count):
    current = strain
    level_list = []
    for rate_level in range(count):
        if rate_level > 0:
            paired = current.reshape(current.shape[0], -1, 2)
            current = (paired[:, :, 0] + paired[:, :, 1]) * inv_root_two
        level_list.append(current.astype(jnp.bfloat16))
    return level_list


def filter_level(history, rounded, basis_bf, stride):
    tap_rows = basis_bf[::stride]
    joined = jnp.concatenate([history[:, 1:], rounded], axis=1)
    return lax.conv_general_dilated(
        joined[:, :, None],
        tap_rows[::-1][:, None, :],
        (1,),
        "VALID",
        dimension_numbers=("NWC", "WIO", "NWC"),
        preferred_element_type=jnp.float32,
    )


def basis_from(product):
    inner_gram = jnp.dot(product.T, product, precision=highest)
    lower_factor = jnp.linalg.cholesky(inner_gram)
    basis_bf = jax.scipy.linalg.solve_triangular(lower_factor, product.T, lower=True).T.astype(
        jnp.bfloat16
    )
    return (basis_bf, jnp.diagonal(lower_factor))


def local(templates, owner_device, rate_code, rate_gains, sketch, strain):
    tpl_rows = templates.shape[0]
    slice_len = templates.shape[1]
    group_size = lax.axis_size("grp")
    bin_count = lax.axis_size("bin")
    devices = bin_count * group_size
    capacity = 2 * tpl_rows // devices
    scale_down = tpl_rows * group_size * math.sqrt(slice_len)
    whitened = whiten_rows(templates, rate_code, rate_gains)
    target = owner_device[:, 0]
    member_table = (target[:, None] == jnp.arange(devices, dtype=jnp.int32)[None, :]).astype(
        jnp.int32
    )
    rank_in_dest = jnp.sum(jnp.cumsum(member_table, axis=0) * member_table, axis=1) - 1
    slot_index = target * capacity + rank_in_dest
    outgoing = jnp.zeros((devices * capacity, slice_len), jnp.bfloat16).at[slot_index].set(whitened)
    received = lax.all_to_all(outgoing, ("bin", "grp"), split_axis=0, concat_axis=0, tiled=True)
    partial_gram = lax.dot_general(
        received, received, (((0,), (0,)), ((), ())), preferred_element_type=jnp.float32
    )
    gram_total = lax.psum(partial_gram, "grp")
    product = jnp.dot(gram_total, sketch, precision=highest)
    basis_bf, diag_here = basis_from(product)
    coeffs = jnp.dot(received, basis_bf, preferred_element_type=jnp.float32).astype(jnp.bfloat16)
    returned = lax.all_to_all(coeffs, ("bin", "grp"), split_axis=0, concat_axis=0, tiled=True)
    mixing = returned[slot_index]
    spectrum = (diag_here / scale_down)[None, :]
    levels = strain_levels(strain, rate_gains.shape[0])
    rim_list = [
        levels[rate_level][:, -(slice_len >> rate_level) :] for rate_level in range(len(levels))
    ]
    history = shifted((rim_list[0], rim_list[1], rim_list[2], rim_list[3], rim_list[4]), "grp", 1)
    filtered = []
    for rate_level in range(len(levels)):
        result_level = filter_level(
            history[rate_level], levels[rate_level], basis_bf, 2**rate_level
        )
        filtered.append(result_level.astype(jnp.bfloat16)[None])
    return (mixing, spectrum, filtered[0], filtered[1], filtered[2], filtered[3], filtered[4])


def solution(mesh):
    return jax.shard_map(
        local,
        mesh=mesh,
        in_specs=(
            P(("bin", "grp"), None),
            P(("bin", "grp"), None),
            P(("bin", "grp")),
            P(),
            P(),
            P(None, "grp"),
        ),
        out_specs=(
            P(("bin", "grp"), None),
            P("bin", None),
            P("bin", None, "grp", None),
            P("bin", None, "grp", None),
            P("bin", None, "grp", None),
            P("bin", None, "grp", None),
            P("bin", None, "grp", None),
        ),
        check_vma=False,
    )
```

profile of v0, /device:TPU:1, one launch (start us, length us, event | category | flops | bytes accessed | tf_op | source)
XLA Modules:
  0.0 488.1 jit_solution(5350892277837483940)
XLA Ops:
  9.0 7.3 %scatter_custom_fusion = bf16[2048,512]{1,0:T(8,128)(2,1)} fusion(s32[1024]{0:T(1024)S(1)} %bitcast.143, bf16[1024,512]{1,0:T(8,128)(2,1)S(1)} %copy-done.3, f32[512]{0:T(512)S(1)} %bitcast.149, f32[512]{0:T(512)S(1)} %bitcast.150, f32[512]{0:T(512)S(1)} %bitcast.147, f32[512]{0:T(512)S(1)} %bitcast.148, f32[]{:T(128)} %constant.105.clone.1, ...), kind=kCustom, calls=%fused_computation.26 | custom fusion | flops 6291456 | bytes 3161094 | tf_op jit(solution)/shard_map/scatter | solution.py:74
  16.3 12.0 %all-to-all-start = ((bf16[128,16,512]{2,1,0:T(8,128)(2,1)}), bf16[128,16,512]{2,1,0:T(8,128)(2,1)}, u32[]{:S(2)}, u32[]{:S(2)}) async-start(bf16[128,16,512]{2,1,0:T(8,128)(2,1)} %bitcast.12), calls=%async_computation | async-start | bytes 4194304 | tf_op jit(solution)/shard_map/all_to_all | solution.py:75
  28.4 3.7 collective-permute-start
  32.1 6.4 %reshape.114 = f32[2,4096,2]{2,1,0:T(8,128)} reshape(f32[2,8192]{1,0:T(2,128)S(1)} %copy-done.6) | data formatting | bytes 131072 | tf_op jit(solution)/shard_map/reshape | solution.py:31
  38.5 5.9 %convert_reduce_fusion = bf16[2,4096]{1,0:T(2,128)(2,1)S(1)} fusion(f32[2,4096,2]{2,1,0:T(8,128)} %reshape.114), kind=kLoop, calls=%fused_computation.17 | loop fusion | flops 24576 | bytes 81920 | tf_op jit(solution)/shard_map/convert_element_type | solution.py:33
  44.4 2.2 collective-permute-start.1
  46.7 2.4 fusion.3
  49.0 2.2 mul.59
  52.4 3.6 collective-permute-start.2
  62.7 3.3 collective-permute-start.4
  71.7 4.5 convolution_bitcast_fusion
  78.0 104.7 %all-reduce.3.cloned.1.call-done = f32[512,512]{1,0:T(8,128)} async-done(((f32[512,512]{1,0:T(8,128)}), f32[512,512]{1,0:T(8,128)}) %all-reduce.3.cloned.1.call-update) | async-done | bytes 1048592 | tf_op jit(solution)/shard_map/psum | solution.py:79
  182.7 2.2 fusion.55
  186.2 11.7 %cholesky.50 = f32[128,128]{1,0:T(8,128)S(1)} custom-call(f32[128,128]{1,0:T(8,128)S(1)} %cholesky.118), custom_call_target="Cholesky" | custom-call | tf_op jit(solution)/shard_map/jit(cholesky)/cholesky | solution.py:52
  197.9 9.8 %custom-call.15 = f32[1,128,128]{1,2,0:T(8,128)S(1)} custom-call(f32[1,128,128]{2,1,0:T(8,128)S(1)} %get-tuple-element.30), custom_call_target="InvertDiagBlocksLowerTriangular" | custom-call | tf_op jit(solution)/shard_map/jit(cholesky)/cholesky | solution.py:52
  208.2 12.2 %cholesky.105 = f32[128,128]{1,0:T(8,128)S(1)} custom-call(f32[128,128]{1,0:T(8,128)S(1)} %convolution_subtract_fusion.1), custom_call_target="Cholesky" | custom-call | tf_op jit(solution)/shard_map/jit(cholesky)/cholesky | solution.py:52
  222.5 4.0 while.1
  226.5 19.7 %custom-call.16 = f32[2,128,128]{1,2,0:T(8,128)S(1)} custom-call(f32[2,128,128]{2,1,0:T(8,128)S(1)} %get-tuple-element.14), custom_call_target="InvertDiagBlocksLowerTriangular" | custom-call | tf_op jit(solution)/shard_map/jit(_solve_triangular)/triangular_solve | solution.py:53
  248.5 6.6 %slice.147 = bf16[256,256]{0,1:T(8,128)(2,1)} slice(bf16[512,256]{0,1:T(8,128)(2,1)S(1)} %fusion.31), slice={[0:512:2], [0:256:1]} | slice | bytes 262144 | tf_op jit(solution)/shard_map/slice | solution.py:38
  255.1 3.0 slice.152
  261.3 3.3 convolution_convert_fusion
  264.6 8.5 %all-to-all-start.1 = ((bf16[128,16,256]{2,1,0:T(8,128)(2,1)}), bf16[128,16,256]{2,1,0:T(8,128)(2,1)}, u32[]{:S(2)}, u32[]{:S(2)}) async-start(bf16[128,16,256]{2,1,0:T(8,128)(2,1)} %bitcast.21), calls=%async_computation.1 | async-start | bytes 2097152 | tf_op jit(solution)/shard_map/all_to_all | solution.py:83
  273.1 2.3 gather_fusion.1
  276.4 123.6 %select_convert_fusion = bf16[16,1088,256]{2,0,1:T(8,128)(2,1)} fusion(pred[16,1088]{0,1:T(8,128)(4,1)S(1)} %bitcast.152, bf16[16,1599,1]{0,2,1:T(2,128)(2,1)S(1)} %copy.25, bf16[512,1,256]{2,1,0:T(2,128)(2,1)S(1)} %copy.26), kind=kOutput, calls=%fused_computation.5 | convolution fusion | flops 4572315648 | bytes 9243616 | tf_op jit(solution)/shard_map/conv_general_dilated | solution.py:40
  400.1 10.2 %copy.27 = bf16[16,1088,256]{2,1,0:T(8,128)(2,1)} copy(bf16[16,1088,256]{2,0,1:T(8,128)(2,1)} %select_convert_fusion) | data formatting | bytes 17825792 | tf_op jit(solution)/shard_map/convert_element_type | solution.py:96
  410.3 7.4 %slice_bitcast_fusion = bf16[1,2,8192,256]{3,2,1,0:T(8,128)(2,1)} fusion(bf16[2,8704,256]{2,1,0:T(8,128)(2,1)} %bitcast.129), kind=kLoop, calls=%fused_computation.7 | loop fusion | bytes 16777216 | tf_op jit(solution)/shard_map/broadcast_in_dim | solution.py:96
  418.3 31.3 %select_convert_fusion.1 = bf16[16,544,256]{2,0,1:T(8,128)(2,1)S(1)} fusion(pred[16,544]{0,1:T(8,128)(4,1)S(1)} %bitcast.153, bf16[16,799,1]{0,2,1:T(2,128)(2,1)S(1)} %copy-done.5, bf16[256,1,256]{2,1,0:T(2,128)(2,1)S(1)} %copy.29), kind=kOutput, calls=%fused_computation.6 | convolution fusion | flops 1145307136 | bytes 4621792 | tf_op jit(solution)/shard_map/conv_general_dilated | solution.py:40
  449.6 3.6 copy.30
  453.6 8.4 %select_convert_fusion.2 = bf16[16,272,256]{2,0,1:T(8,128)(2,1)S(1)} fusion(pred[16,272]{0,1:T(8,128)(4,1)S(1)} %copy-done.19, bf16[16,399,1]{0,2,1:T(2,128)(2,1)S(1)} %copy-done.10, bf16[128,1,256]{2,1,0:T(2,128)(2,1)S(1)} %copy.32), kind=kOutput, calls=%fused_computation.8 | convolution fusion | flops 287440896 | bytes 2310880 | tf_op jit(solution)/shard_map/conv_general_dilated | solution.py:40
  464.6 2.5 select_convert_fusion.3
  470.6 4.5 slice_bitcast_fusion.1
  475.0 6.0 %gather_fusion = bf16[1024,256]{1,0:T(8,128)(2,1)} fusion(bf16[2048,256]{1,0:T(8,128)(2,1)} %bitcast.22, s32[1024]{0:T(1024)S(1)} %copy-done.14), kind=kCustom, calls=%fused_computation | custom fusion | bytes 1052672 | tf_op jit(solution)/shard_map/gather | solution.py:84
  (161 shorter events, 37.0 us)
Async XLA Ops:
  7.2 175.5 %copy-start = (f32[512,256]{1,0:T(8,128)S(1)}, f32[512,256]{1,0:T(8,128)}, u32[]{:S(2)}) copy-start(f32[512,256]{1,0:T(8,128)} %param.10) | copy-start | bytes 1572868
  7.2 1.3 copy-start.13
  7.2 1.7 copy-start.15
  7.2 1.8 copy-start.16
  7.2 1.8 copy-start.3
  16.3 12.0 %copy-start.6 = (f32[2,8192]{1,0:T(2,128)S(1)}, f32[2,8192]{1,0:T(2,128)}, u32[]{:S(2)}) copy-start(f32[2,8192]{1,0:T(2,128)} %param.11) | copy-start | bytes 196612
  16.3 55.3 %all-to-all-start = ((bf16[128,16,512]{2,1,0:T(8,128)(2,1)}), bf16[128,16,512]{2,1,0:T(8,128)(2,1)}, u32[]{:S(2)}, u32[]{:S(2)}) async-start(bf16[128,16,512]{2,1,0:T(8,128)(2,1)} %bitcast.12), calls=%async_computation | async-start | bytes 4194304 | tf_op jit(solution)/shard_map/all_to_all | solution.py:75
  28.3 154.4 %all-reduce.3.cloned.1.call-start = ((), (), s32[]{:S(2)}) async-start(), calls=%async_computation.2 | async-start | bytes 2097152 | tf_op jit(solution)/shard_map/psum | solution.py:79
  28.4 43.2 %collective-permute-start = (bf16[2,512]{1,0:T(2,128)(2,1)S(1)}, bf16[2,512]{1,0:T(2,128)(2,1)S(1)}, u32[]{:S(2)}, u32[]{:S(2)}) collective-permute-start(bf16[2,512]{1,0:T(2,128)(2,1)S(1)} %slice.190), channel_id=1, source_target_pairs={{0,1},{1,2},{2,3},{3,4},{4,5},{5,6},{6,7},{7,8},{8,9},{9,10},{10,1... | collective-permute-start | bytes 6152 | tf_op jit(solution)/shard_map/ppermute | solution.py:14
  38.5 8.1 %copy-start.2 = (f32[2,4096,2]{2,1,0:T(8,128)S(1)}, f32[2,4096,2]{2,1,0:T(8,128)}, u32[]{:S(2)}) copy-start(f32[2,4096,2]{2,1,0:T(8,128)} %reshape.114) | copy-start | bytes 196612
  44.4 25.7 %collective-permute-start.1 = (bf16[2,256]{1,0:T(2,128)(2,1)S(1)}, bf16[2,256]{1,0:T(2,128)(2,1)S(1)}, u32[]{:S(2)}, u32[]{:S(2)}) collective-permute-start(bf16[2,256]{1,0:T(2,128)(2,1)S(1)} %slice.196), channel_id=1, source_target_pairs={{0,1},{1,2},{2,3},{3,4},{4,5},{5,6},{6,7},{7,8},{8,9},{9,10},{10,1... | collective-permute-start | bytes 3080 | tf_op jit(solution)/shard_map/ppermute | solution.py:14
  52.4 16.5 %collective-permute-start.2 = (bf16[2,128]{1,0:T(2,128)(2,1)S(1)}, bf16[2,128]{1,0:T(2,128)(2,1)S(1)}, u32[]{:S(2)}, u32[]{:S(2)}) collective-permute-start(bf16[2,128]{1,0:T(2,128)(2,1)S(1)} %slice.202), channel_id=1, source_target_pairs={{0,1},{1,2},{2,3},{3,4},{4,5},{5,6},{6,7},{7,8},{8,9},{9,10},{10,1... | collective-permute-start | bytes 1544 | tf_op jit(solution)/shard_map/ppermute | solution.py:14
  59.0 8.8 %collective-permute-start.3 = (bf16[2,64]{1,0:T(2,128)(2,1)S(1)}, bf16[2,64]{1,0:T(2,128)(2,1)S(1)}, u32[]{:S(2)}, u32[]{:S(2)}) collective-permute-start(bf16[2,64]{1,0:T(2,128)(2,1)S(1)} %slice.207), channel_id=1, source_target_pairs={{0,1},{1,2},{2,3},{3,4},{4,5},{5,6},{6,7},{7,8},{8,9},{9,10},{10,1... | collective-permute-start | bytes 776 | tf_op jit(solution)/shard_map/ppermute | solution.py:14
  62.7 4.0 collective-permute-start.4
  264.6 11.8 %copy-start.17 = (pred[16,1088]{0,1:T(32,128)(4,1)S(1)}, pred[16,1088]{0,1:T(32,128)(4,1)}, u32[]{:S(2)}) copy-start(pred[16,1088]{0,1:T(32,128)(4,1)} %constant.152) | copy-start | bytes 52228
  264.6 210.4 %all-to-all-start.1 = ((bf16[128,16,256]{2,1,0:T(8,128)(2,1)}), bf16[128,16,256]{2,1,0:T(8,128)(2,1)}, u32[]{:S(2)}, u32[]{:S(2)}) async-start(bf16[128,16,256]{2,1,0:T(8,128)(2,1)} %bitcast.21), calls=%async_computation.1 | async-start | bytes 2097152 | tf_op jit(solution)/shard_map/all_to_all | solution.py:83
  410.3 7.4 %copy-start.4 = (bf16[256,256]{0,1:T(8,128)(2,1)S(1)}, bf16[256,256]{0,1:T(8,128)(2,1)}, u32[]{:S(2)}) copy-start(bf16[256,256]{0,1:T(8,128)(2,1)} %slice.147) | copy-start | bytes 393220
  410.3 8.0 %copy-start.5 = (bf16[16,799,1]{0,2,1:T(2,128)(2,1)S(1)}, bf16[16,799,1]{0,2,1:T(2,128)(2,1)}, u32[]{:S(2)}) copy-start(bf16[16,799,1]{0,2,1:T(2,128)(2,1)} %copy.28) | copy-start | bytes 76708
  410.3 8.0 %copy-start.18 = (pred[16,544]{0,1:T(32,128)(4,1)S(1)}, pred[16,544]{0,1:T(32,128)(4,1)}, u32[]{:S(2)}) copy-start(pred[16,544]{0,1:T(32,128)(4,1)} %constant.153) | copy-start | bytes 26116
  449.6 3.7 copy-start.9
  449.6 4.0 copy-start.10
  449.6 4.0 copy-start.19
  462.7 1.5 copy-start.8
  462.7 1.8 copy-start.11
  462.8 1.8 copy-start.20
  467.0 1.4 copy-start.7
  467.0 1.7 copy-start.12
  467.0 1.7 copy-start.21
  470.6 4.5 copy-start.14
  475.0 6.0 %copy-start.1 = (f32[512,256]{1,0:T(8,128)S(1)}, f32[512,256]{1,0:T(8,128)}, u32[]{:S(2)}) copy-start(f32[512,256]{1,0:T(8,128)} %param.10) | copy-start | bytes 1572868
Sparse Core Ops, SparseCore 0:
  76.3 106.3 all-reduce.2
where the time goes:
time: 496 us; the launch traced here: 488 us
  matrix products  179 us (36%)
  waiting for transfers between devices  105 us (21%)
  other arithmetic  76.5 us (15%)
  local copies, waits for them, and re-layouts  75.8 us (15%)
  starting transfers between devices  35.3 us (7%)
  between operations  16.3 us (3%)
    conv_general_dilated x5, matrix products, filter_level(): lax.conv_general_dilated(joined[:, :, None], tap_rows[::-1][:, None, :],...  166 us
    psum x1, waiting for transfers between devices, local(): gram_total = lax.psum(partial_gram, 'grp')  105 us
    another operation x6, other arithmetic, basis_from(): lower_factor = jnp.linalg.cholesky(inner_gram)  34.4 us
    another operation x3, other arithmetic, basis_from(): jax.scipy.linalg.solve_triangular(lower_factor, product.T, lower=True)  19.7 us
    convert_element_type x6, local copies, waits for them, and re-layouts, local(): filtered.append(result_level.astype(jnp.bfloat16)[None])  15.2 us
    broadcast_in_dim x5, local copies, waits for them, and re-layouts, local(): filtered.append(result_level.astype(jnp.bfloat16)[None])  15.2 us
    ppermute x5, starting transfers between devices, shifted(): return lax.ppermute(x, axis, pairs)  14.9 us
    slice x4, local copies, waits for them, and re-layouts, filter_level(): tap_rows = basis_bf[::stride]  12.8 us
  transfers between devices with their start and end apart: 8, of which 2 were waited for; matrix products, arithmetic and copies ran while one was open for 47% of the time, Pallas kernels for 0%

commit v1 on v0

--- a/solution.py
+++ b/solution.py
@@ -76,7 +76,8 @@
     partial_gram = lax.dot_general(
         received, received, (((0,), (0,)), ((), ())), preferred_element_type=jnp.float32
     )
-    gram_total = lax.psum(partial_gram, "grp")
+    parts = lax.all_gather(partial_gram, "grp", axis=0, tiled=False)
+    gram_total = parts.sum(axis=0)
     product = jnp.dot(gram_total, sketch, precision=highest)
     basis_bf, diag_here = basis_from(product)
     coeffs = jnp.dot(received, basis_bf, preferred_element_type=jnp.float32).astype(jnp.bfloat16)

time: 496 us -> 501 us (1.010)
  blocking collectives: 0 us -> 41.7 us
  waiting for transfers between devices: 105 us -> 77.4 us
  starting transfers between devices: 35.3 us -> 20.3 us
  other arithmetic: 76.5 us -> 91.2 us
    psum x1 -> x0, waiting for transfers between devices: 105 us -> none  [local(): gram_total = lax.psum(partial_gram, 'grp')]
    all_gather x0 -> x1, waiting for transfers between devices: none -> 65.6 us  [local(): parts = lax.all_gather(partial_gram, 'grp', axis=0, tiled=False)]
    all_to_all x0 -> x1, blocking collectives: none -> 41.7 us  [local(): lax.all_to_all(outgoing, ('bin', 'grp'), split_axis=0, concat_axis=0, til...]
    reduce_sum x0 -> x1, other arithmetic: none -> 12.3 us  [local(): gram_total = parts.sum(axis=0)]
    all_to_all x1 -> x0, starting transfers between devices: 12 us -> none  [local(): lax.all_to_all(outgoing, ('bin', 'grp'), split_axis=0, concat_axis=0, til...]
    all_to_all x1, waiting for transfers between devices: 0.01 us -> 11.8 us  [local(): lax.all_to_all(coeffs, ('bin', 'grp'), split_axis=0, concat_axis=0, tiled...]
    mul x3, other arithmetic: 4.24 us -> 9.64 us  [strain_levels(): current = (paired[:, :, 0] + paired[:, :, 1]) * inv_root_two]
  transfers between devices with their start and end apart: 8 -> 7, of which waited for: 2 -> 2; matrix products, arithmetic and copies ran while one was open for 47% -> 8% of each run, Pallas kernels for 0% -> 0%
where the time goes in v1:
time: 501 us; the launch traced here: 496 us
  matrix products  174 us (35%)
  other arithmetic  91.2 us (18%)
  waiting for transfers between devices  77.4 us (15%)
  local copies, waits for them, and re-layouts  75.8 us (15%)
  blocking collectives  41.7 us (8%)
  starting transfers between devices  20.3 us (4%)
  between operations  16.4 us (3%)
    conv_general_dilated x5, matrix products, filter_level(): lax.conv_general_dilated(joined[:, :, None], tap_rows[::-1][:, None, :],...  166 us
    all_gather x1, waiting for transfers between devices, local(): parts = lax.all_gather(partial_gram, 'grp', axis=0, tiled=False)  65.6 us
    all_to_all x1, blocking collectives, local(): lax.all_to_all(outgoing, ('bin', 'grp'), split_axis=0, concat_axis=0, til...  41.7 us
    another operation x6, other arithmetic, basis_from(): lower_factor = jnp.linalg.cholesky(inner_gram)  34 us
    another operation x3, other arithmetic, basis_from(): jax.scipy.linalg.solve_triangular(lower_factor, product.T, lower=True)  20.4 us
    convert_element_type x6, local copies, waits for them, and re-layouts, local(): filtered.append(result_level.astype(jnp.bfloat16)[None])  15.4 us
    broadcast_in_dim x5, local copies, waits for them, and re-layouts, local(): filtered.append(result_level.astype(jnp.bfloat16)[None])  15.3 us
    ppermute x5, starting transfers between devices, shifted(): return lax.ppermute(x, axis, pairs)  13.2 us
  transfers between devices with their start and end apart: 7, of which 2 were waited for; matrix products, arithmetic and copies ran while one was open for 8% of the time, Pallas kernels for 0%

profile of v1, /device:TPU:1, one launch (start us, length us, event | category | flops | bytes accessed | tf_op | source)
XLA Modules:
  0.0 496.3 jit_solution(10699770187401592794)
XLA Ops:
  9.0 6.9 %scatter_custom_fusion = bf16[2048,512]{1,0:T(8,128)(2,1)S(1)} fusion(s32[1024]{0:T(1024)S(1)} %bitcast.148, bf16[1024,512]{1,0:T(8,128)(2,1)} %param.6, f32[512]{0:T(512)S(1)} %bitcast.154, f32[512]{0:T(512)S(1)} %bitcast.155, f32[512]{0:T(512)S(1)} %bitcast.152, f32[512]{0:T(512)S(1)} %bitcast.153, f32[]{:T(128)} %constant.105.clone.1, ...), kind=kCustom, calls=%fused_computation.26 | custom fusion | flops 6291456 | bytes 3161094 | tf_op jit(solution)/shard_map/scatter | solution.py:74
  15.9 41.7 %all_to_all.24 = bf16[128,16,512]{2,1,0:T(8,128)(2,1)S(1)} all-to-all(bf16[128,16,512]{2,1,0:T(8,128)(2,1)S(1)} %bitcast.136), channel_id=1, replica_groups=mesh['bin'=4,'grp'=32] {'bin','grp'}, dimensions={0} | all-to-all | bytes 4194304 | tf_op jit(solution)/shard_map/all_to_all | solution.py:75
  59.0 2.3 convolution_bitcast_fusion
  61.3 6.4 %reshape.114 = f32[2,4096,2]{2,1,0:T(8,128)} reshape(f32[2,8192]{1,0:T(2,128)S(1)} %copy-done.14) | data formatting | bytes 131072 | tf_op jit(solution)/shard_map/reshape | solution.py:31
  67.7 6.2 %fusion.3 = f32[2,4096]{1,0:T(2,128)S(1)} fusion(f32[2,4096,2]{2,1,0:T(8,128)} %reshape.114), kind=kLoop, calls=%fused_computation.25 | loop fusion | flops 16384 | bytes 98304 | tf_op jit(solution)/shard_map/mul | solution.py:32
  79.3 2.2 fusion.24
  82.5 3.2 collective-permute-start.4
  89.8 2.3 collective-permute-start.2
  92.2 2.4 convert_reduce_fusion
  96.5 3.5 collective-permute-start
  106.1 65.6 %all-gather.3.cloned.1.call-done = f32[16384,512]{1,0:T(8,128)} async-done(((f32[512,512]{1,0:T(8,128)}), f32[16384,512]{1,0:T(8,128)}) %all-gather.3.cloned.1.call-update) | async-done | bytes 33554448 | tf_op jit(solution)/shard_map/all_gather | solution.py:79
  171.7 12.3 %reduce_sum.19 = f32[512,512]{1,0:T(8,128)S(1)} reduce(f32[32,512,512]{2,1,0:T(8,128)} %bitcast.131, f32[]{:T(128)} %constant.105.clone.1), dimensions={0}, to_apply=%region_4.5 | reduce | flops 8126464 | bytes 34603012 | tf_op jit(solution)/shard_map/reduce_sum | solution.py:80
  186.2 11.7 %cholesky.50 = f32[128,128]{1,0:T(8,128)S(1)} custom-call(f32[128,128]{1,0:T(8,128)S(1)} %cholesky.118), custom_call_target="Cholesky" | custom-call | tf_op jit(solution)/shard_map/jit(cholesky)/cholesky | solution.py:52
  198.0 9.8 %custom-call.15 = f32[1,128,128]{1,2,0:T(8,128)S(1)} custom-call(f32[1,128,128]{2,1,0:T(8,128)S(1)} %get-tuple-element.30), custom_call_target="InvertDiagBlocksLowerTriangular" | custom-call | tf_op jit(solution)/shard_map/jit(cholesky)/cholesky | solution.py:52
  208.3 11.8 %cholesky.105 = f32[128,128]{1,0:T(8,128)S(1)} custom-call(f32[128,128]{1,0:T(8,128)S(1)} %convolution_subtract_fusion.1), custom_call_target="Cholesky" | custom-call | tf_op jit(solution)/shard_map/jit(cholesky)/cholesky | solution.py:52
  222.8 4.0 while.1
  226.9 19.7 %custom-call.16 = f32[2,128,128]{1,2,0:T(8,128)S(1)} custom-call(f32[2,128,128]{2,1,0:T(8,128)S(1)} %get-tuple-element.14), custom_call_target="InvertDiagBlocksLowerTriangular" | custom-call | tf_op jit(solution)/shard_map/jit(_solve_triangular)/triangular_solve | solution.py:53
  250.7 2.4 slice.152
  253.1 6.1 %slice.147 = bf16[256,256]{0,1:T(8,128)(2,1)S(1)} slice(bf16[512,256]{0,1:T(8,128)(2,1)S(1)} %fusion.31), slice={[0:512:2], [0:256:1]} | slice | bytes 262144 | tf_op jit(solution)/shard_map/slice | solution.py:38
  259.2 2.9 rev.15
  264.6 2.5 select_convert_fusion.3
  268.9 8.6 %select_convert_fusion.2 = bf16[16,272,256]{2,0,1:T(8,128)(2,1)S(1)} fusion(pred[16,272]{0,1:T(8,128)(4,1)S(1)} %copy-done.21, bf16[16,399,1]{0,2,1:T(2,128)(2,1)S(1)} %copy.56, bf16[128,1,256]{2,1,0:T(2,128)(2,1)S(1)} %copy.57), kind=kOutput, calls=%fused_computation.8 | convolution fusion | flops 287440896 | bytes 2310880 | tf_op jit(solution)/shard_map/conv_general_dilated | solution.py:40
  280.3 31.3 %select_convert_fusion.1 = bf16[16,544,256]{2,0,1:T(8,128)(2,1)S(1)} fusion(pred[16,544]{0,1:T(8,128)(4,1)S(1)} %bitcast.158, bf16[16,799,1]{0,2,1:T(2,128)(2,1)S(1)} %copy.53, bf16[256,1,256]{2,1,0:T(2,128)(2,1)S(1)} %copy.54), kind=kOutput, calls=%fused_computation.6 | convolution fusion | flops 1145307136 | bytes 4621792 | tf_op jit(solution)/shard_map/conv_general_dilated | solution.py:40
  311.6 3.8 copy.55
  315.9 122.7 %select_convert_fusion = bf16[16,1088,256]{2,0,1:T(8,128)(2,1)} fusion(pred[16,1088]{0,1:T(8,128)(4,1)S(1)} %bitcast.157, bf16[16,1599,1]{0,2,1:T(2,128)(2,1)S(1)} %copy-done.9, bf16[512,1,256]{2,1,0:T(2,128)(2,1)S(1)} %copy.51), kind=kOutput, calls=%fused_computation.5 | convolution fusion | flops 4572315648 | bytes 9243616 | tf_op jit(solution)/shard_map/conv_general_dilated | solution.py:40
  438.6 10.2 %copy.52 = bf16[16,1088,256]{2,1,0:T(8,128)(2,1)} copy(bf16[16,1088,256]{2,0,1:T(8,128)(2,1)} %select_convert_fusion) | data formatting | bytes 17825792 | tf_op jit(solution)/shard_map/convert_element_type | solution.py:97
  448.8 7.5 %slice_bitcast_fusion = bf16[1,2,8192,256]{3,2,1,0:T(8,128)(2,1)} fusion(bf16[2,8704,256]{2,1,0:T(8,128)(2,1)} %bitcast.130), kind=kLoop, calls=%fused_computation.7 | loop fusion | bytes 16777216 | tf_op jit(solution)/shard_map/broadcast_in_dim | solution.py:97
  458.0 7.1 %all-to-all-start.1 = ((bf16[128,16,256]{2,1,0:T(8,128)(2,1)}), bf16[128,16,256]{2,1,0:T(8,128)(2,1)S(1)}, u32[]{:S(2)}, u32[]{:S(2)}) async-start(bf16[128,16,256]{2,1,0:T(8,128)(2,1)} %bitcast.22), calls=%async_computation.1 | async-start | bytes 2097152 | tf_op jit(solution)/shard_map/all_to_all | solution.py:84
  465.1 2.3 gather_fusion.1
  468.0 4.5 slice_bitcast_fusion.1
  472.5 11.8 %all-to-all-done.1 = bf16[128,16,256]{2,1,0:T(8,128)(2,1)S(1)} async-done(((bf16[128,16,256]{2,1,0:T(8,128)(2,1)}), bf16[128,16,256]{2,1,0:T(8,128)(2,1)S(1)}, u32[]{:S(2)}, u32[]{:S(2)}) %all-to-all-start.1) | async-done | bytes 1048608 | tf_op jit(solution)/shard_map/all_to_all | solution.py:84
  484.2 5.0 %gather_fusion = bf16[1024,256]{1,0:T(8,128)(2,1)} fusion(bf16[2048,256]{1,0:T(8,128)(2,1)S(1)} %bitcast.132, s32[1024]{0:T(1024)S(1)} %copy-done.16), kind=kCustom, calls=%fused_computation | custom fusion | bytes 1052672 | tf_op jit(solution)/shard_map/gather | solution.py:85
  (165 shorter events, 43.4 us)
Async XLA Ops:
  7.2 176.8 %copy-start = (f32[512,256]{1,0:T(8,128)S(1)}, f32[512,256]{1,0:T(8,128)}, u32[]{:S(2)}) copy-start(f32[512,256]{1,0:T(8,128)} %param.10) | copy-start | bytes 1572868
  7.2 1.3 copy-start.15
  7.2 1.7 copy-start.17
  7.2 1.7 copy-start.18
  7.2 164.5 %all-gather.3.cloned.1.call-start = ((), (), s32[]{:S(2)}) async-start(), calls=%async_computation.2 | async-start | bytes 34603008 | tf_op jit(solution)/shard_map/all_gather | solution.py:79
  57.7 1.3 copy-start.6
  59.0 2.3 copy-start.14
  82.0 3.7 copy-start.3
  82.5 18.8 %collective-permute-start.4 = (bf16[2,32]{1,0:T(2,128)(2,1)S(1)}, bf16[2,32]{1,0:T(2,128)(2,1)S(1)}, u32[]{:S(2)}, u32[]{:S(2)}) collective-permute-start(bf16[2,32]{1,0:T(2,128)(2,1)S(1)} %slice.212), channel_id=1, source_target_pairs={{0,1},{1,2},{2,3},{3,4},{4,5},{5,6},{6,7},{7,8},{8,9},{9,10},{10,1... | collective-permute-start | bytes 392 | tf_op jit(solution)/shard_map/ppermute | solution.py:14
  86.4 5.7 %copy-start.2 = (f32[2,4096,2]{2,1,0:T(8,128)S(1)}, f32[2,4096,2]{2,1,0:T(8,128)}, u32[]{:S(2)}) copy-start(f32[2,4096,2]{2,1,0:T(8,128)} %reshape.114) | copy-start | bytes 196612
  86.4 15.3 %collective-permute-start.3 = (bf16[2,64]{1,0:T(2,128)(2,1)S(1)}, bf16[2,64]{1,0:T(2,128)(2,1)S(1)}, u32[]{:S(2)}, u32[]{:S(2)}) collective-permute-start(bf16[2,64]{1,0:T(2,128)(2,1)S(1)} %slice.207), channel_id=1, source_target_pairs={{0,1},{1,2},{2,3},{3,4},{4,5},{5,6},{6,7},{7,8},{8,9},{9,10},{10,1... | collective-permute-start | bytes 776 | tf_op jit(solution)/shard_map/ppermute | solution.py:14
  89.8 12.4 %collective-permute-start.2 = (bf16[2,128]{1,0:T(2,128)(2,1)S(1)}, bf16[2,128]{1,0:T(2,128)(2,1)S(1)}, u32[]{:S(2)}, u32[]{:S(2)}) collective-permute-start(bf16[2,128]{1,0:T(2,128)(2,1)S(1)} %slice.202), channel_id=1, source_target_pairs={{0,1},{1,2},{2,3},{3,4},{4,5},{5,6},{6,7},{7,8},{8,9},{9,10},{10,1... | collective-permute-start | bytes 1544 | tf_op jit(solution)/shard_map/ppermute | solution.py:14
  94.5 8.2 %collective-permute-start.1 = (bf16[2,256]{1,0:T(2,128)(2,1)S(1)}, bf16[2,256]{1,0:T(2,128)(2,1)S(1)}, u32[]{:S(2)}, u32[]{:S(2)}) collective-permute-start(bf16[2,256]{1,0:T(2,128)(2,1)S(1)} %slice.196), channel_id=1, source_target_pairs={{0,1},{1,2},{2,3},{3,4},{4,5},{5,6},{6,7},{7,8},{8,9},{9,10},{10,1... | collective-permute-start | bytes 3080 | tf_op jit(solution)/shard_map/ppermute | solution.py:14
  96.5 7.3 %collective-permute-start = (bf16[2,512]{1,0:T(2,128)(2,1)S(1)}, bf16[2,512]{1,0:T(2,128)(2,1)S(1)}, u32[]{:S(2)}, u32[]{:S(2)}) collective-permute-start(bf16[2,512]{1,0:T(2,128)(2,1)S(1)} %slice.190), channel_id=1, source_target_pairs={{0,1},{1,2},{2,3},{3,4},{4,5},{5,6},{6,7},{7,8},{8,9},{9,10},{10,1... | collective-permute-start | bytes 6152 | tf_op jit(solution)/shard_map/ppermute | solution.py:14
  226.8 35.6 %copy-start.23 = (pred[16,68]{0,1:T(8,128)(4,1)S(1)}, pred[16,68]{0,1:T(8,128)(4,1)}, u32[]{:S(2)}) copy-start(pred[16,68]{0,1:T(8,128)(4,1)} %constant.156) | copy-start | bytes 3268
  247.0 1.0 copy-start.12
  248.0 0.7 copy-start.10
  263.1 1.4 copy-start.22
  267.1 1.8 copy-start.21
  278.2 2.1 copy-start.20
  311.6 3.8 copy-start.8
  311.6 4.2 copy-start.9
  311.6 4.2 copy-start.19
  448.8 7.5 %copy-start.7 = (bf16[128,16,512]{2,1,0:T(8,128)(2,1)S(1)}, bf16[128,16,512]{2,1,0:T(8,128)(2,1)}, u32[]{:S(2)}) copy-start(bf16[128,16,512]{2,1,0:T(8,128)(2,1)} %copy-done.6) | copy-start | bytes 6291460
  448.8 7.5 %copy-start.11 = (bf16[128,512]{1,0:T(8,128)(2,1)S(1)}, bf16[128,512]{1,0:T(8,128)(2,1)}, u32[]{:S(2)}) copy-start(bf16[128,512]{1,0:T(8,128)(2,1)} %copy-done.10) | copy-start | bytes 393220
  448.8 7.5 %copy-start.13 = (bf16[128,512]{1,0:T(8,128)(2,1)S(1)}, bf16[128,512]{1,0:T(8,128)(2,1)}, u32[]{:S(2)}) copy-start(bf16[128,512]{1,0:T(8,128)(2,1)} %copy-done.12) | copy-start | bytes 393220
  458.0 7.1 %copy-start.4 = (s32[256,1]{0,1:T(1,128)S(1)}, s32[256,1]{0,1:T(1,128)}, u32[]{:S(2)}) copy-start(s32[256,1]{0,1:T(1,128)} %shift-left_or_fusion) | copy-start | bytes 3076
  458.0 7.1 %copy-start.5 = (f32[256,256]{1,0:T(8,128)S(1)}, f32[256,256]{1,0:T(8,128)}, u32[]{:S(2)}) copy-start(f32[256,256]{1,0:T(8,128)} %get-tuple-element.24) | copy-start | bytes 786436
  458.0 26.2 %all-to-all-start.1 = ((bf16[128,16,256]{2,1,0:T(8,128)(2,1)}), bf16[128,16,256]{2,1,0:T(8,128)(2,1)S(1)}, u32[]{:S(2)}, u32[]{:S(2)}) async-start(bf16[128,16,256]{2,1,0:T(8,128)(2,1)} %bitcast.22), calls=%async_computation.1 | async-start | bytes 2097152 | tf_op jit(solution)/shard_map/all_to_all | solution.py:84
  468.0 16.2 %copy-start.16 = (s32[1024]{0:T(1024)S(1)}, s32[1024]{0:T(1024)}, u32[]{:S(2)}) copy-start(s32[1024]{0:T(1024)} %broadcast_clamp_fusion) | copy-start | bytes 12292
  484.2 5.0 %copy-start.1 = (f32[512,256]{1,0:T(8,128)S(1)}, f32[512,256]{1,0:T(8,128)}, u32[]{:S(2)}) copy-start(f32[512,256]{1,0:T(8,128)} %param.10) | copy-start | bytes 1572868
Sparse Core Ops, SparseCore 0:
  61.4 110.2 all-gather.2
